TPU v7x, 32 devices: a whole 2x2x4 slice. The times are simulated.
32 devices in a mesh: pairs: 8 (over z, x), grp: 4 (over y, core).
Axes of the slice: x: 2, y: 2, z: 4, core: 2. Of those that a mesh axis runs over, the one named last changes fastest.
Arguments:
- coefficients: bfloat16 [128, 512, 128], P('pairs', 'grp'), may hold values from -0.4140625 to 0.4140625
- domain: int32 [128, 512], P('pairs', 'grp'), may hold values from 0 to 767, as said below
- coupling_owner: int32 [128, 8], P('pairs'), may hold values from 0 to 7, all different within a row; in each aligned block of 16 rows (0 to 15, 16 to 31, ...) at most 16 rows name the same one
- coupling_slot: int32 [128, 8], P('pairs'), may hold values from 0 to 15
- coupling_fock: float32 [128, 8], P('pairs'), may hold values from -0.5 to 0.5
- exchange_integrals: float32 [128, 128, 128], P('pairs'), may hold values from -6 to 6
- pno_energy: float32 [128, 128], P('pairs'), may hold values from 0.3 to 3
- pair_shift: float32 [128], P('pairs'), may hold values from 0.4 to 2
- amplitudes_start: float32 [128, 128, 128], P('pairs'), may hold values from -1.8 to 1.8
Outputs:
- amplitudes: float32 [128, 128, 128], P('pairs')
Inputs may be any that keep to these rules, and one draw needn't show every extreme that they name: `coupling_owner`: each row names different indices. Among the 16 rows of one index of pairs no value is named more than 16 times, a bound that some block reaches. `domain`: for each pair and each g from 0 to 3, the entries g * 128 to (g + 1) * 128 - 1 are distinct numbers from g * 192 to (g + 1) * 192 - 1.
All inputs are finite; a program needn't handle non-finite values.
Results may differ from a plain program's by a relative error of at most 0.0025.
Values may be sent and summed in bfloat16 or wider, within the bound.
A program may use at most 128 MiB of HBM per device.

v0:
```python
import jax
import jax.numpy as jnp
from jax import lax
from jax.sharding import PartitionSpec as P

NB = 192
ITERS = 2


def on_device(
    coefficients,
    domain,
    coupling_owner,
    coupling_slot,
    coupling_fock,
    exchange_integrals,
    pno_energy,
    pair_shift,
    amplitudes_start,
):
    pair_count = coefficients.shape[0]
    block_rows = coefficients.shape[1]
    pno_count = coefficients.shape[2]
    link_count = coupling_owner.shape[1]
    pair_ranks = lax.axis_size("pairs")
    capacity = min(pair_count, (pair_count * link_count + pair_ranks - 1) // pair_ranks + 1)
    group_index = lax.axis_index("grp")
    local_dom = domain - group_index * NB
    owners = coupling_owner.T.reshape(-1)
    slots = coupling_slot.T.reshape(-1)
    owner_hits = (owners[:, None] == jnp.arange(pair_ranks, dtype=jnp.int32)[None, :]).astype(
        jnp.int32
    )
    earlier = jnp.cumsum(owner_hits, axis=0) - owner_hits
    link_rank = jnp.sum(earlier * owner_hits, axis=1)
    slot_hits = owner_hits[:, :, None] * (
        link_rank[:, None, None] == jnp.arange(capacity, dtype=jnp.int32)[None, None, :]
    ).astype(jnp.int32)
    request = jnp.sum(slot_hits * slots[:, None, None], axis=0)
    wanted = lax.all_to_all(request, "pairs", split_axis=0, concat_axis=0, tiled=True).reshape(-1)
    position = owners * capacity + link_rank
    outgoing_rows = jnp.take(coefficients, wanted, axis=0).reshape(
        pair_ranks, capacity, block_rows, pno_count
    )
    outgoing_dom = jnp.take(local_dom, wanted, axis=0).reshape(pair_ranks, capacity, block_rows)
    incoming_rows = lax.all_to_all(outgoing_rows, "pairs", split_axis=0, concat_axis=0, tiled=True)
    incoming_dom = lax.all_to_all(outgoing_dom, "pairs", split_axis=0, concat_axis=0, tiled=True)
    source_rows = jnp.take(
        incoming_rows.reshape(pair_ranks * capacity, block_rows, pno_count), position, axis=0
    )
    source_rows = source_rows.reshape(link_count, pair_count, block_rows, pno_count)
    source_dom = jnp.take(incoming_dom.reshape(pair_ranks * capacity, block_rows), position, axis=0)
    source_dom = source_dom.reshape(link_count, pair_count, block_rows)
    match = (local_dom[None, :, :, None] == source_dom[:, :, None, :]).astype(jnp.bfloat16)
    gathered = jnp.einsum(
        "kprs,kpsc->kprc", match, source_rows, preferred_element_type=jnp.float32
    ).astype(jnp.bfloat16)
    position_links = position.reshape(link_count, pair_count)
    fock_links = coupling_fock.T
    intersection = lax.psum(
        jnp.einsum("pra,kprc->kpac", coefficients, gathered, preferred_element_type=jnp.float32),
        "grp",
    )
    intersection_half = intersection.astype(jnp.bfloat16)
    used_links = intersection_half.shape[0]
    denominator = pno_energy[:, :, None] + pno_energy[:, None, :] + pair_shift[:, None, None]
    amplitudes = amplitudes_start
    for iteration in range(ITERS):
        sendable = amplitudes.astype(jnp.bfloat16)
        outgoing_amp = jnp.take(sendable, wanted, axis=0).reshape(
            pair_ranks, capacity, pno_count, pno_count
        )
        incoming_amp = lax.all_to_all(
            outgoing_amp, "pairs", split_axis=0, concat_axis=0, tiled=True
        )
        source_amp = jnp.take(
            incoming_amp.reshape(pair_ranks * capacity, pno_count, pno_count),
            position_links.reshape(-1),
            axis=0,
        )
        source_amp = source_amp.reshape(used_links, pair_count, pno_count, pno_count)
        half_proj = jnp.einsum(
            "kpac,kpcd->kpad", intersection_half, source_amp, preferred_element_type=jnp.float32
        ).astype(jnp.bfloat16)
        projected = jnp.einsum(
            "kpad,kpbd->kpab", half_proj, intersection_half, preferred_element_type=jnp.float32
        )
        coupled = jnp.sum(fock_links[:, :, None, None] * projected, axis=0)
        amplitudes = -(exchange_integrals + coupled) / denominator
    return amplitudes


def solution(mesh):
    placed = (
        P("pairs", "grp", None),
        P("pairs", "grp"),
        P("pairs", None),
        P("pairs", None),
        P("pairs", None),
        P("pairs", None, None),
        P("pairs", None),
        P("pairs"),
        P("pairs", None, None),
    )
    return jax.shard_map(
        on_device, mesh=mesh, in_specs=placed, out_specs=P("pairs", None, None), check_vma=False
    )
```

profile of v0, /device:TPU:0, one launch (start us, length us, event | category | flops | bytes accessed | tf_op | source)
XLA Modules:
  0.0 524.1 jit_solution(13798727091787789117)
XLA Ops:
  0.0 0.0 copy-start
  0.0 0.8 reshape.197
  0.8 0.8 mul.76
  1.6 0.1 fusion.43
  1.7 0.2 reduce_window_sum.11
  1.9 0.2 select_reduce_fusion
  2.1 0.8 multiply_reduce_fusion.2
  2.9 7.3 %all-to-all-start = ((s32[8,1,16]{2,1,0:T(1,128)}), s32[8,1,16]{2,1,0:T(1,128)S(1)}, u32[]{:S(2)}, u32[]{:S(2)}) async-start(s32[8,1,16]{2,1,0:T(1,128)} %bitcast.4), calls=%async_computation | async-start | bytes 8192 | tf_op jit(solution)/shard_map/all_to_all | solution.py:40
  10.2 0.7 broadcast_subtract_fusion
  10.9 1.3 convert_element_type.38
  12.2 4.4 all-to-all-done
  16.6 0.1 reshape.201
  16.8 0.5 broadcast.152
  17.3 0.7 reduce.5
  17.9 0.1 reshape.199
  18.0 0.6 gather_fusion
  18.7 0.7 broadcast_select_fusion.7
  19.4 3.4 all-to-all-start.1
  22.8 3.0 gather_fusion.4
  25.8 0.0 copy-done
  25.8 3.1 gather_fusion.2
  28.8 6.0 %broadcast_select_fusion.3 = (bf16[128,128,128]{2,1,0:T(8,128)(2,1)}, bf16[128,128,128]{2,1,0:T(8,128)(2,1)}) fusion(bf16[128,128,128]{2,1,0:T(8,128)(2,1)} %gather_fusion.4, pred[128]{0:T(512)(128)(4,1)S(1)} %compare_and_fusion.3, bf16[128,128,128]{2,1,0:T(8,128)(2,1)} %gather_fusion.2), kind=kLoop, calls=%fused_computation.24 | loop fusion | flops 4194304 | bytes 16777344 | tf_op jit(solution)/shard_map/jit(_take)/select_n | solution.py:70
  34.8 0.0 all-to-all-done.1
  34.8 97.5 %all_to_all.29 = bf16[8,16,128,128]{3,2,1,0:T(8,128)(2,1)} all-to-all(bf16[8,16,128,128]{3,2,1,0:T(8,128)(2,1)} %bitcast.41), channel_id=1, replica_groups=mesh['pairs'=8,'grp'=4] {'pairs'}, dimensions={0} | all-to-all | bytes 8388608 | tf_op jit(solution)/shard_map/all_to_all | solution.py:46
  132.3 0.0 copy-start.4
  132.3 4.7 all-to-all-start.3
  137.0 0.1 reduce_sum.41
  137.1 0.0 copy-done.4
  137.1 0.1 mul.80
  137.2 0.6 gather_fusion.1
  137.9 0.1 broadcast_select_fusion.6
  138.0 5.2 gather_fusion.3
  143.2 85.8 %all-to-all-done.3 = bf16[8,16,128,128]{3,2,1,0:T(8,128)(2,1)} async-done(((bf16[8,16,128,128]{3,2,1,0:T(8,128)(2,1)}), bf16[8,16,128,128]{3,2,1,0:T(8,128)(2,1)}, u32[]{:S(2)}, u32[]{:S(2)}) %all-to-all-start.3) | async-done | bytes 4194336 | tf_op jit(solution)/shard_map/all_to_all | solution.py:73
  229.1 5.2 %gather_fusion.5 = bf16[128,128,128]{2,1,0:T(8,128)(2,1)} fusion(bf16[128,128,128]{2,1,0:T(8,128)(2,1)} %bitcast.19, s32[1024]{0:T(1024)S(1)} %pad_clamp_fusion), kind=kCustom, calls=%fused_computation.4.clone | custom fusion | bytes 8389120 | tf_op jit(solution)/shard_map/jit(_take)/gather | solution.py:76
  234.3 6.0 %broadcast_select_fusion = (bf16[128,128,128]{2,1,0:T(8,128)(2,1)}, bf16[128,128,128]{2,1,0:T(8,128)(2,1)}) fusion(bf16[128,128,128]{2,1,0:T(8,128)(2,1)} %gather_fusion.5, pred[128]{0:T(512)(128)(4,1)S(1)} %get-tuple-element.6, bf16[128,128,128]{2,1,0:T(8,128)(2,1)} %gather_fusion.3), kind=kLoop, calls=%fused_computation.21 | loop fusion | flops 4194304 | bytes 16777344 | tf_op jit(solution)/shard_map/jit(_take)/select_n | solution.py:76
  240.3 6.5 %fusion.11 = f32[8,16,128,128]{2,3,0,1:T(8,128)} fusion(bf16[8,16,128,128]{3,2,1,0:T(8,128)(2,1)} %bitcast.43, s32[8,16,128]{2,0,1:T(8,128)S(1)} %copy.25, s32[16,128]{1,0:T(8,128)S(1)} %broadcast_subtract_fusion, bf16[16,128,128]{2,1,0:T(8,128)(2,1)S(1)} %copy-done), kind=kOutput, calls=%fused_computation.27 | convolution fusion | flops 1077936128 | bytes 13180928 | tf_op jit(solution)/shard_map/pra,kprc->kpac/dot_general | solution.py:61
  246.8 0.0 copy-start.6
  246.8 146.3 %all-reduce.1 = bf16[8,16,128,128]{2,3,0,1:T(8,128)(2,1)} all-reduce(f32[8,16,128,128]{2,3,0,1:T(8,128)} %fusion.11), channel_id=1, replica_groups=mesh['pairs'=8,'grp'=4] {'grp'}, use_global_device_ids=true, to_apply=%region_3.6 | all-reduce | flops 2097152 | bytes 12582912 | tf_op jit(solution)/shard_map/psum | solution.py:60
  393.1 0.0 copy-done.6
  393.1 0.0 copy-start.2
  393.1 0.0 copy-start.3
  393.1 0.0 copy-start.5
  393.1 7.5 %multiply_reduce_fusion.1 = f32[16,128,128]{2,1,0:T(8,128)S(1)} fusion(f32[8,16]{1,0:T(8,128)S(1)} %bitcast.55, bf16[8,16,128,128]{2,3,0,1:T(8,128)(2,1)} %all-reduce.1, bf16[8,16,128,128]{3,2,1,0:T(8,128)(2,1)} %bitcast.47), kind=kOutput, calls=%fused_computation.9 | convolution fusion | flops 1079771136 | bytes 9437696 | tf_op jit(solution)/shard_map/kpad,kpbd->kpab/dot_general | solution.py:85
  400.6 0.0 copy-done.2
  400.6 0.0 copy-done.3
  400.6 0.0 copy-done.5
  400.6 0.4 divide_convert_fusion
  401.1 3.0 gather_fusion.6
  404.1 2.6 broadcast_select_fusion.4
  406.7 98.7 %all_to_all.30 = bf16[8,16,128,128]{3,2,1,0:T(8,128)(2,1)} all-to-all(bf16[8,16,128,128]{3,2,1,0:T(8,128)(2,1)S(1)} %bitcast.44), channel_id=1, replica_groups=mesh['pairs'=8,'grp'=4] {'pairs'}, dimensions={0} | all-to-all | bytes 8388608 | tf_op jit(solution)/shard_map/all_to_all | solution.py:73
  505.4 5.2 %gather_fusion.7 = bf16[128,128,128]{2,1,0:T(8,128)(2,1)} fusion(bf16[128,128,128]{2,1,0:T(8,128)(2,1)} %bitcast.45, s32[1024]{0:T(1024)S(1)} %pad_clamp_fusion), kind=kCustom, calls=%fused_computation.5.clone | custom fusion | bytes 8389120 | tf_op jit(solution)/shard_map/jit(_take)/gather | solution.py:76
  510.6 4.6 broadcast_select_fusion.1
  515.2 0.0 copy-start.1
  515.2 7.5 %multiply_reduce_fusion = f32[16,128,128]{2,1,0:T(8,128)S(1)} fusion(f32[8,16]{1,0:T(8,128)S(1)} %bitcast.56, bf16[8,16,128,128]{2,3,0,1:T(8,128)(2,1)} %all-reduce.1, bf16[8,16,128,128]{3,2,1,0:T(8,128)(2,1)} %bitcast.48), kind=kOutput, calls=%fused_computation.8 | convolution fusion | flops 1079771136 | bytes 9437696 | tf_op jit(solution)/shard_map/kpad,kpbd->kpab/dot_general | solution.py:85
  522.7 1.4 negate_divide_fusion
  524.1 0.0 copy-done.1
  (15 shorter events, 0.2 us)
Async XLA Ops:
  0.0 25.8 %copy-start = (bf16[16,128,128]{2,1,0:T(8,128)(2,1)S(1)}, bf16[16,128,128]{2,1,0:T(8,128)(2,1)}, u32[]{:S(2)}) copy-start(bf16[16,128,128]{2,1,0:T(8,128)(2,1)} %param.13) | copy-start | bytes 1572868
  2.9 13.7 %all-to-all-start = ((s32[8,1,16]{2,1,0:T(1,128)}), s32[8,1,16]{2,1,0:T(1,128)S(1)}, u32[]{:S(2)}, u32[]{:S(2)}) async-start(s32[8,1,16]{2,1,0:T(1,128)} %bitcast.4), calls=%async_computation | async-start | bytes 8192 | tf_op jit(solution)/shard_map/all_to_all | solution.py:40
  19.4 15.4 %all-to-all-start.1 = ((s32[8,16,128]{2,1,0:T(8,128)}), s32[8,16,128]{2,1,0:T(8,128)S(1)}, u32[]{:S(2)}, u32[]{:S(2)}) async-start(s32[8,16,128]{2,1,0:T(8,128)} %broadcast_select_fusion.7), calls=%async_computation.1 | async-start | bytes 131072 | tf_op jit(solution)/shard_map/all_to_all | solution.py:47
  132.3 4.8 copy-start.4
  132.3 96.7 %all-to-all-start.3 = ((bf16[8,16,128,128]{3,2,1,0:T(8,128)(2,1)}), bf16[8,16,128,128]{3,2,1,0:T(8,128)(2,1)}, u32[]{:S(2)}, u32[]{:S(2)}) async-start(bf16[8,16,128,128]{3,2,1,0:T(8,128)(2,1)} %bitcast.40), calls=%async_computation.3 | async-start | bytes 8388608 | tf_op jit(solution)/shard_map/all_to_all | solution.py:73
  246.8 146.3 %copy-start.6 = (f32[16,8]{0,1:T(8,128)S(1)}, f32[16,8]{0,1:T(8,128)}, u32[]{:S(2)}) copy-start(f32[16,8]{0,1:T(8,128)} %param.17) | copy-start | bytes 1540
  393.1 7.5 %copy-start.2 = (f32[16,128,128]{2,1,0:T(8,128)S(1)}, f32[16,128,128]{2,1,0:T(8,128)}, u32[]{:S(2)}) copy-start(f32[16,128,128]{2,1,0:T(8,128)} %param.18) | copy-start | bytes 3145732
  393.1 7.5 %copy-start.3 = (f32[16,128]{1,0:T(8,128)S(1)}, f32[16,128]{1,0:T(8,128)}, u32[]{:S(2)}) copy-start(f32[16,128]{1,0:T(8,128)} %param.19) | copy-start | bytes 24580
  393.1 7.5 %copy-start.5 = (f32[16]{0:T(128)S(1)}, f32[16]{0:T(128)}, u32[]{:S(2)}) copy-start(f32[16]{0:T(128)} %param.20) | copy-start | bytes 196
  515.2 8.9 %copy-start.1 = (bf16[16,128,128]{2,1,0:T(8,128)(2,1)S(1)}, bf16[16,128,128]{2,1,0:T(8,128)(2,1)}, u32[]{:S(2)}) copy-start(bf16[16,128,128]{2,1,0:T(8,128)(2,1)} %param.13) | copy-start | bytes 1572868
where the time goes:
time: 525 us; the launch traced here: 524 us
  blocking collectives  342 us (65%)
  waiting for transfers between devices  90.2 us (17%)
  local copies, waits for them, and re-layouts  28.6 us (5%)
  other arithmetic  25.8 us (5%)
  matrix products  21.5 us (4%)
  starting transfers between devices  15.3 us (3%)
    psum x1, blocking collectives, on_device(): lax.psum(jnp.einsum('pra,kprc->kpac', coefficients, gathered, preferred_e...  146 us
    all_to_all x1, blocking collectives, on_device(): lax.all_to_all(outgoing_amp, 'pairs', split_axis=0, concat_axis=0, tiled=...  98.7 us
    all_to_all x1, blocking collectives, on_device(): lax.all_to_all(outgoing_rows, 'pairs', split_axis=0, concat_axis=0, tiled...  97.5 us
    all_to_all x1, waiting for transfers between devices, on_device(): lax.all_to_all(outgoing_amp, 'pairs', split_axis=0, concat_axis=0, tiled=...  85.8 us
    dot_general x2, matrix products, on_device(): jnp.einsum('kpad,kpbd->kpab', half_proj, intersection_half, preferred_ele...  15 us
    select_n x2, other arithmetic, on_device(): jnp.take(incoming_amp.reshape(pair_ranks * capacity, pno_count, pno_count...  10.6 us
  transfers between devices with their start and end apart: 3, of which 2 were waited for; matrix products, arithmetic and copies ran while one was open for 4% of the time, Pallas kernels for 0%

commit v1 on v0

--- a/solution.py
+++ b/solution.py
@@ -57,10 +57,9 @@
     ).astype(jnp.bfloat16)
     position_links = position.reshape(link_count, pair_count)
     fock_links = coupling_fock.T
-    intersection = lax.psum(
-        jnp.einsum("pra,kprc->kpac", coefficients, gathered, preferred_element_type=jnp.float32),
-        "grp",
-    )
+    x = jnp.einsum("pra,kprc->kpac", coefficients, gathered, preferred_element_type=jnp.float32)
+    pieces = lax.all_gather(x, "grp", axis=0, tiled=False)
+    intersection = pieces.sum(axis=0)
     intersection_half = intersection.astype(jnp.bfloat16)
     used_links = intersection_half.shape[0]
     denominator = pno_energy[:, :, None] + pno_energy[:, None, :] + pair_shift[:, None, None]

time: 525 us -> 608 us (1.16)
  waiting for transfers between devices: 90.2 us -> 291 us
  blocking collectives: 342 us -> 196 us
  other arithmetic: 25.8 us -> 40.9 us
  between operations: 0.2 us -> 13.6 us
    all_gather x0 -> x1, waiting for transfers between devices: none -> 201 us  [on_device(): pieces = lax.all_gather(x, 'grp', axis=0, tiled=False)]
    psum x1 -> x0, blocking collectives: 146 us -> none  [on_device(): lax.psum(jnp.einsum('pra,kprc->kpac', coefficients, gathered, preferred_e...]
    reduce_sum x0 -> x1, other arithmetic: none -> 15.2 us  [on_device(): intersection = pieces.sum(axis=0)]
  transfers between devices with their start and end apart: 3 -> 4, of which waited for: 2 -> 3; matrix products, arithmetic and copies ran while one was open for 4% -> 3% of each run, Pallas kernels for 0% -> 0%
where the time goes in v1:
time: 608 us; the launch traced here: 607 us
  waiting for transfers between devices  291 us (48%)
  blocking collectives  196 us (32%)
  other arithmetic  40.9 us (7%)
  local copies, waits for them, and re-layouts  28.6 us (5%)
  matrix products  21.4 us (4%)
  starting transfers between devices  15.5 us (3%)
  between operations  13.6 us (2%)
    all_gather x1, waiting for transfers between devices, on_device(): pieces = lax.all_gather(x, 'grp', axis=0, tiled=False)  201 us
    all_to_all x1, blocking collectives, on_device(): lax.all_to_all(outgoing_amp, 'pairs', split_axis=0, concat_axis=0, tiled=...  99 us
    all_to_all x1, blocking collectives, on_device(): lax.all_to_all(outgoing_rows, 'pairs', split_axis=0, concat_axis=0, tiled...  97.5 us
    all_to_all x1, waiting for transfers between devices, on_device(): lax.all_to_all(outgoing_amp, 'pairs', split_axis=0, concat_axis=0, tiled=...  85.6 us
    reduce_sum x1, other arithmetic, on_device(): intersection = pieces.sum(axis=0)  15.2 us
    dot_general x2, matrix products, on_device(): jnp.einsum('kpad,kpbd->kpab', half_proj, intersection_half, preferred_ele...  14.9 us
  transfers between devices with their start and end apart: 4, of which 3 were waited for; matrix products, arithmetic and copies ran while one was open for 3% of the time, Pallas kernels for 0%

profile of v1, /device:TPU:0, one launch (start us, length us, event | category | flops | bytes accessed | tf_op | source)
XLA Modules:
  0.0 607.3 jit_solution(4861316663578787842)
XLA Ops:
  6.5 0.0 copy-start
  6.5 0.8 reshape.197
  7.4 0.8 mul.76
  8.1 0.1 fusion.43
  8.3 0.2 reduce_window_sum.11
  8.5 0.2 select_reduce_fusion
  8.7 0.8 multiply_reduce_fusion.2
  9.5 7.3 %all-to-all-start = ((s32[8,1,16]{2,1,0:T(1,128)}), s32[8,1,16]{2,1,0:T(1,128)S(1)}, u32[]{:S(2)}, u32[]{:S(2)}) async-start(s32[8,1,16]{2,1,0:T(1,128)} %bitcast.4), calls=%async_computation | async-start | bytes 8192 | tf_op jit(solution)/shard_map/all_to_all | solution.py:40
  16.8 0.7 broadcast_subtract_fusion
  17.4 1.3 convert_element_type.38
  18.8 4.4 all-to-all-done
  23.2 0.1 reshape.201
  23.3 0.5 broadcast.152
  23.8 0.7 reduce.5
  24.5 0.1 reshape.199
  24.6 0.6 gather_fusion
  25.2 0.7 broadcast_select_fusion.7
  25.9 3.4 all-to-all-start.1
  29.3 3.0 gather_fusion.4
  32.3 0.0 copy-done
  32.3 3.1 gather_fusion.2
  35.4 6.0 broadcast_select_fusion.3
  41.3 0.0 all-to-all-done.1
  41.3 97.5 %all_to_all.29 = bf16[8,16,128,128]{3,2,1,0:T(8,128)(2,1)} all-to-all(bf16[8,16,128,128]{3,2,1,0:T(8,128)(2,1)} %bitcast.43), channel_id=1, replica_groups=mesh['pairs'=8,'grp'=4] {'pairs'}, dimensions={0} | all-to-all | bytes 8388608 | tf_op jit(solution)/shard_map/all_to_all | solution.py:46
  138.9 0.0 copy-start.4
  138.9 4.7 all-to-all-start.3
  143.5 0.2 all-gather.3.cloned.1.call-start
  143.8 0.1 reduce_sum.50
  143.8 0.0 copy-done.4
  143.9 0.1 mul.80
  144.0 0.6 gather_fusion.1
  144.7 0.1 broadcast_select_fusion.6
  144.8 5.2 gather_fusion.3
  150.0 85.6 %all-to-all-done.3 = bf16[8,16,128,128]{3,2,1,0:T(8,128)(2,1)} async-done(((bf16[8,16,128,128]{3,2,1,0:T(8,128)(2,1)}), bf16[8,16,128,128]{3,2,1,0:T(8,128)(2,1)}, u32[]{:S(2)}, u32[]{:S(2)}) %all-to-all-start.3) | async-done | bytes 4194336 | tf_op jit(solution)/shard_map/all_to_all | solution.py:72
  235.6 5.2 gather_fusion.5
  240.8 6.0 broadcast_select_fusion
  246.8 6.5 %fusion.11 = f32[8,16,128,128]{2,3,0,1:T(8,128)} fusion(bf16[8,16,128,128]{3,2,1,0:T(8,128)(2,1)} %bitcast.45, s32[8,16,128]{2,0,1:T(8,128)S(1)} %copy.23, s32[16,128]{1,0:T(8,128)S(1)} %broadcast_subtract_fusion, bf16[16,128,128]{2,1,0:T(8,128)(2,1)S(1)} %copy-done), kind=kOutput, calls=%fused_computation.27 | convolution fusion | flops 1077936128 | bytes 13180928 | tf_op jit(solution)/shard_map/pra,kprc->kpac/dot_general | solution.py:60
  253.3 0.0 all-gather.3.cloned.1.call-update
  253.3 200.7 %all-gather.3.cloned.1.call-done = f32[32,16,128,128]{2,3,0,1:T(8,128)} async-done(((f32[8,16,128,128]{2,3,0,1:T(8,128)}), f32[32,16,128,128]{2,3,0,1:T(8,128)}) %all-gather.3.cloned.1.call-update) | async-done | bytes 33554448 | tf_op jit(solution)/shard_map/all_gather | solution.py:61
  454.0 0.0 copy-start.6
  454.0 15.2 %reduce_sum.53 = bf16[8,16,128,128]{2,3,0,1:T(8,128)(2,1)} reduce(f32[4,8,16,128,128]{3,4,1,0,2:T(8,128)} %bitcast.41, f32[]{:T(128)} %constant.63.clone.1), dimensions={0}, to_apply=%region_3.6 | reduce | flops 6291456 | bytes 37748740 | tf_op jit(solution)/shard_map/reduce_sum | solution.py:62
  469.3 0.0 copy-done.6
  469.3 0.0 copy-start.2
  469.3 0.0 copy-start.3
  469.3 0.0 copy-start.5
  469.3 7.5 %multiply_reduce_fusion.1 = f32[16,128,128]{2,1,0:T(8,128)S(1)} fusion(f32[8,16]{1,0:T(8,128)S(1)} %bitcast.57, bf16[8,16,128,128]{2,3,0,1:T(8,128)(2,1)} %reduce_sum.53, bf16[8,16,128,128]{3,2,1,0:T(8,128)(2,1)} %bitcast.49), kind=kOutput, calls=%fused_computation.9 | convolution fusion | flops 1079771136 | bytes 9437696 | tf_op jit(solution)/shard_map/kpad,kpbd->kpab/dot_general | solution.py:84
  476.8 0.0 copy-done.2
  476.8 0.0 copy-done.3
  476.8 0.0 copy-done.5
  476.8 0.4 divide_convert_fusion
  477.2 3.0 gather_fusion.6
  480.2 2.6 broadcast_select_fusion.4
  482.8 99.0 %all_to_all.30 = bf16[8,16,128,128]{3,2,1,0:T(8,128)(2,1)} all-to-all(bf16[8,16,128,128]{3,2,1,0:T(8,128)(2,1)S(1)} %bitcast.46), channel_id=1, replica_groups=mesh['pairs'=8,'grp'=4] {'pairs'}, dimensions={0} | all-to-all | bytes 8388608 | tf_op jit(solution)/shard_map/all_to_all | solution.py:72
  581.8 5.2 gather_fusion.7
  587.0 4.6 broadcast_select_fusion.1
  591.6 0.0 copy-start.1
  591.6 7.4 %multiply_reduce_fusion = f32[16,128,128]{2,1,0:T(8,128)S(1)} fusion(f32[8,16]{1,0:T(8,128)S(1)} %bitcast.58, bf16[8,16,128,128]{2,3,0,1:T(8,128)(2,1)} %reduce_sum.53, bf16[8,16,128,128]{3,2,1,0:T(8,128)(2,1)} %bitcast.50), kind=kOutput, calls=%fused_computation.8 | convolution fusion | flops 1079771136 | bytes 9437696 | tf_op jit(solution)/shard_map/kpad,kpbd->kpab/dot_general | solution.py:84
  599.1 1.3 negate_divide_fusion
  600.4 0.0 copy-done.1
  (15 shorter events, 0.2 us)
Async XLA Ops:
  6.5 25.8 %copy-start = (bf16[16,128,128]{2,1,0:T(8,128)(2,1)S(1)}, bf16[16,128,128]{2,1,0:T(8,128)(2,1)}, u32[]{:S(2)}) copy-start(bf16[16,128,128]{2,1,0:T(8,128)(2,1)} %param.13) | copy-start | bytes 1572868
  9.5 13.7 %all-to-all-start = ((s32[8,1,16]{2,1,0:T(1,128)}), s32[8,1,16]{2,1,0:T(1,128)S(1)}, u32[]{:S(2)}, u32[]{:S(2)}) async-start(s32[8,1,16]{2,1,0:T(1,128)} %bitcast.4), calls=%async_computation | async-start | bytes 8192 | tf_op jit(solution)/shard_map/all_to_all | solution.py:40
  25.9 15.4 %all-to-all-start.1 = ((s32[8,16,128]{2,1,0:T(8,128)}), s32[8,16,128]{2,1,0:T(8,128)S(1)}, u32[]{:S(2)}, u32[]{:S(2)}) async-start(s32[8,16,128]{2,1,0:T(8,128)} %broadcast_select_fusion.7), calls=%async_computation.1 | async-start | bytes 131072 | tf_op jit(solution)/shard_map/all_to_all | solution.py:47
  138.9 5.0 copy-start.4
  138.9 96.7 %all-to-all-start.3 = ((bf16[8,16,128,128]{3,2,1,0:T(8,128)(2,1)}), bf16[8,16,128,128]{3,2,1,0:T(8,128)(2,1)}, u32[]{:S(2)}, u32[]{:S(2)}) async-start(bf16[8,16,128,128]{3,2,1,0:T(8,128)(2,1)} %bitcast.42), calls=%async_computation.3 | async-start | bytes 8388608 | tf_op jit(solution)/shard_map/all_to_all | solution.py:72
  143.5 310.5 %all-gather.3.cloned.1.call-start = ((), (), s32[]{:S(2)}) async-start(), calls=%async_computation.5 | async-start | bytes 41943040 | tf_op jit(solution)/shard_map/all_gather | solution.py:61
  454.0 15.2 %copy-start.6 = (f32[16,8]{0,1:T(8,128)S(1)}, f32[16,8]{0,1:T(8,128)}, u32[]{:S(2)}) copy-start(f32[16,8]{0,1:T(8,128)} %param.17) | copy-start | bytes 1540
  469.3 7.5 %copy-start.2 = (f32[16,128,128]{2,1,0:T(8,128)S(1)}, f32[16,128,128]{2,1,0:T(8,128)}, u32[]{:S(2)}) copy-start(f32[16,128,128]{2,1,0:T(8,128)} %param.18) | copy-start | bytes 3145732
  469.3 7.5 %copy-start.3 = (f32[16,128]{1,0:T(8,128)S(1)}, f32[16,128]{1,0:T(8,128)}, u32[]{:S(2)}) copy-start(f32[16,128]{1,0:T(8,128)} %param.19) | copy-start | bytes 24580
  469.3 7.5 %copy-start.5 = (f32[16]{0:T(128)S(1)}, f32[16]{0:T(128)}, u32[]{:S(2)}) copy-start(f32[16]{0:T(128)} %param.20) | copy-start | bytes 196
  591.6 8.8 %copy-start.1 = (bf16[16,128,128]{2,1,0:T(8,128)(2,1)S(1)}, bf16[16,128,128]{2,1,0:T(8,128)(2,1)}, u32[]{:S(2)}) copy-start(bf16[16,128,128]{2,1,0:T(8,128)(2,1)} %param.13) | copy-start | bytes 1572868
Sparse Core Ops, SparseCore 0:
  253.4 200.5 all-gather.2
